TPU v7x, 32 devices: a whole 2x2x4 slice. The times are simulated.
32 devices in a mesh: grp: 2 (over x), smp: 16 (over z, y, core).
Axes of the slice: x: 2, y: 2, z: 4, core: 2. Of those that a mesh axis runs over, the one named last changes fastest.
Arguments:
- dosage: bfloat16 [2048, 4096], P('smp', 'grp'), parts along dimension 1, may hold values from 0.008 to 4.5, as said below
- flags: int32 [256], P('grp'), parts along dimension 0, may hold values from 0 to 2047, as said below
- events: int32 [2048, 32], P('smp', 'grp'), parts along dimension 1, may hold values from 0 to 1, as said below
- offsets: float32 [2048, 32], P('smp', 'grp'), parts along dimension 1, may hold values from -3 to 3
Outputs:
- effect: float32 [16, 256], P(None, 'grp'), parts along dimension 1
- zscore: float32 [16, 256], P(None, 'grp'), parts along dimension 1
There are 2 independent parts, one for each index of `grp`. A program takes and returns all parts, laid end to end along the dimension named above; each array names one. Nothing has to cross between parts.
Inputs may be any that keep to these rules, and one draw needn't show every extreme that they name: `flags`: 128 distinct column numbers in rising order, the first 0 and the last 2047. `events`: 0 or 1; every endpoint has an event at the first sample. `dosage`: positive dosages.
All inputs are finite; a program needn't handle non-finite values.
Results may differ from a plain program's by a relative error of at most 0.0013.
Values sent between devices are 32-bit elements; how exact they have to be, the bound alone decides.
A program may use at most 64 MiB of HBM per device.

v0:
```python
import functools

import jax
import jax.numpy as jnp
from jax import lax
from jax.experimental import pallas as pl
from jax.experimental.pallas import tpu as pltpu
from jax.sharding import PartitionSpec as P

ITERS = 3
SUB = 8
GROUP = 5
MESH = pl.DeviceIdType.MESH
F32 = jnp.float32
BF16 = jnp.bfloat16


def thirds(x):
    high = x.astype(BF16).astype(F32)
    rest = x - high
    middle = rest.astype(BF16).astype(F32)
    return high, middle, rest - middle


def transposed_dot(a, b):
    return lax.dot_general(a, b, (((0,), (0,)), ((), ())), preferred_element_type=F32)


def iota(shape, dim):
    return lax.broadcasted_iota(jnp.int32, shape, dim)


def kernel(
    n, flags_hbm, dosage_hbm, offsets_hbm, events_hbm, out_ref,
    flags_ref, dosage_ref, offsets_ref, events_ref,
    send, recv, dose_ref, shift_ref, mark_ref, weight_ref, totals, carries, rsend, rrecv,
    load_sem, send_sem, recv_sem, rsend_sem, rrecv_sem,
):
    me = lax.axis_index("smp")
    rows, columns = dosage_ref.shape
    endpoints = offsets_ref.shape[0]
    part = endpoints // 2
    variants = flags_ref.shape[1]
    own = variants * 2 // n
    lanes = dose_ref.shape[1]
    steps = rows // SUB

    loads = [
        pltpu.make_async_copy(src, dst, load_sem.at[at])
        for at, (src, dst) in enumerate(
            ((flags_hbm, flags_ref), (dosage_hbm, dosage_ref), (offsets_hbm, offsets_ref), (events_hbm, events_ref))
        )
    ]
    for load in loads:
        load.start()

    barrier = pltpu.get_barrier_semaphore()

    def peer(step):
        return lax.rem(me + step, n)

    @pl.loop(1, n)
    def _(step):
        pl.semaphore_signal(barrier, inc=1, device_id={"smp": peer(step)}, device_id_type=MESH)

    line = iota((rows, rows), 1)
    order = (iota((rows, rows), 0) == lax.rem(line, SUB) * steps + lax.div(line, SUB)).astype(F32).astype(BF16)

    loads[2].wait()
    loads[3].wait()
    four = jnp.concatenate([*thirds(offsets_ref[...]), events_ref[...].astype(F32)], axis=0)
    four = jnp.dot(four.astype(BF16), order, preferred_element_type=F32)
    high, middle, low, events = (four[k * endpoints : (k + 1) * endpoints] for k in range(4))
    offsets = (high + middle) + low
    for k in range(n):
        for at, values in ((own, offsets), (own + part, events)):
            send[k, pl.ds(at, part), :] = values[k % 2 * part : (k % 2 + 1) * part]

    loads[0].wait()
    chosen = (iota((columns, variants), 0) == flags_ref[...]).astype(F32).astype(BF16)
    loads[1].wait()
    genotype = jnp.dot(dosage_ref[...], chosen, preferred_element_type=F32).astype(BF16)
    genotype = transposed_dot(genotype, order)
    for k in range(n):
        send[k, pl.ds(0, own), :] = genotype[k // 2 * own : (k // 2 + 1) * own]

    pl.semaphore_wait(barrier, n - 1)

    def copy(at, slot):
        return pltpu.make_async_remote_copy(
            src_ref=send.at[at], dst_ref=recv.at[slot], send_sem=send_sem.at[at], recv_sem=recv_sem.at[slot],
            device_id={"smp": at}, device_id_type=MESH,
        )

    def rcopy(at, slot):
        return pltpu.make_async_remote_copy(
            src_ref=rsend, dst_ref=rrecv.at[slot], send_sem=rsend_sem.at[at], recv_sem=rrecv_sem.at[slot],
            device_id={"smp": at}, device_id_type=MESH,
        )

    @pl.loop(1, n)
    def _(step):
        copy(peer(lax.rem(step + n // 2 - 2, n - 1) + 1), me).start()

    lane_e = iota((part, lanes), 1)
    lane_v = iota((own, lanes), 1)
    spread_e = (lax.div(lane_e, own) == iota((part, lanes), 0)).astype(F32)
    spread_v = jnp.logical_and(lax.rem(lane_v, own) == iota((own, lanes), 0), lane_v < own * part).astype(F32)
    none_e, none_v = jnp.zeros_like(spread_e), jnp.zeros_like(spread_v)
    spread = jnp.concatenate(
        [jnp.concatenate([none_v, none_v, spread_v], axis=1)]
        + [jnp.concatenate([spread_e, none_e, none_e], axis=1)] * 3
        + [jnp.concatenate([none_e, spread_e, none_e], axis=1)],
        axis=0,
    ).astype(BF16)

    def keep(block, sums):
        for k in range(4):
            totals[pl.ds(pl.multiple_of(block * SUB, SUB), SUB), pl.ds(k * lanes, lanes)] = sums[k]

    def add_up(block, slope):
        sums = [jnp.zeros((SUB, lanes), F32)] * 4
        for t in range(steps):
            at = pl.ds(pl.multiple_of(block * rows + t * SUB, SUB), SUB)
            dose = dose_ref[at, :]
            moment = jnp.exp(shift_ref[at, :] + slope * dose)
            weight_ref[at, :] = moment
            for k in range(4):
                sums[k] = sums[k] + moment
                if k < 3:
                    moment = moment * dose
        keep(block, sums)

    def expand(slots, pieces):
        mixed = []
        for values in pieces:
            doses, samples, events = values[:own], values[own : own + part], values[own + part :]
            tall = jnp.concatenate([doses, *thirds(samples), events], axis=0)
            mixed.append(transposed_dot(tall.astype(BF16), spread))
        for slot, values in zip(slots, mixed):
            at = pl.ds(pl.multiple_of(slot * rows, rows), rows)
            shifts, doses = values[:, :lanes], values[:, 2 * lanes :]
            shift_ref[at, :] = shifts
            mark_ref[at, :] = values[:, lanes : 2 * lanes]
            dose_ref[at, :] = doses
            moment = jnp.exp(shifts)
            weight_ref[at, :] = moment
            sums = []
            for k in range(4):
                sums.append(jnp.sum(moment.reshape(steps, SUB, lanes), axis=0))
                if k < 3:
                    moment = moment * doses
            keep(slot, sums)

    expand([me], [send[me]])
    group = max(size for size in range(1, GROUP + 1) if (n - 1) % size == 0)

    @pl.loop(0, (n - 1) // group)
    def _(step):
        slots = [peer(n - 1 - lax.rem(step * group + at + n // 2 - 1, n - 1)) for at in range(group)]
        for slot in slots:
            copy(slot, slot).wait_recv()
        expand(slots, [recv[slot] for slot in slots])

    blocks = n * SUB
    after = (iota((blocks, blocks), 1) > iota((blocks, blocks), 0)).astype(F32).astype(BF16)
    effect = jnp.zeros((1, lanes), F32)
    zscore = effect
    for sweep in range(ITERS):
        if sweep:
            slope = jnp.broadcast_to(effect, (SUB, lanes))

            def again(block, _):
                add_up(block, slope)
                return 0

            lax.fori_loop(0, n, again, 0, unroll=2)
        parts = [
            jnp.dot(after, part.astype(BF16), preferred_element_type=F32) for part in thirds(totals[...])
        ]
        carries[...] = (parts[0] + parts[1]) + parts[2]

        def add_terms(block, sums):
            score, information, skewness = sums
            here = pl.ds(pl.multiple_of(block * SUB, SUB), SUB)
            suffix = [carries[here, pl.ds(k * lanes, lanes)] for k in range(4)]
            for t in reversed(range(steps)):
                at = pl.ds(pl.multiple_of(block * rows + t * SUB, SUB), SUB)
                dose = dose_ref[at, :]
                mark = mark_ref[at, :]
                moment = weight_ref[at, :]
                for k in range(4):
                    suffix[k] = suffix[k] + moment
                    if k < 3:
                        moment = moment * dose
                inverse = 1.0 / suffix[0]
                first = suffix[1] * inverse
                second = suffix[2] * inverse
                third = suffix[3] * inverse
                spread = second - first * first
                score = score + mark * (dose - first)
                information = information + mark * spread
                skewness = skewness + mark * (third - first * (second + (spread + spread)))
            return score, information, skewness

        zero = jnp.zeros((SUB, lanes), F32)
        sums = lax.fori_loop(0, n, add_terms, (zero, zero, zero), unroll=2)
        score, information, skewness = (jnp.sum(x, axis=0, keepdims=True) for x in sums)
        effect = effect + (score + 0.5 * skewness / information) / information
        zscore = effect * jnp.sqrt(information)

    rsend[0:1, :] = effect
    rsend[1:2, :] = zscore

    @pl.loop(1, n)
    def _(step):
        rcopy(peer(step), me).start()

    rrecv[me] = rsend[...]

    @pl.loop(1, n)
    def _(step):
        copy(peer(step), me).wait_send()

    @pl.loop(1, n)
    def _(step):
        rcopy(peer(step), peer(step)).wait_recv()

    out_ref[...] = rrecv[...]

    @pl.loop(1, n)
    def _(step):
        rcopy(peer(step), me).wait_send()


def unfold(n, held, effect_ref, zscore_ref):
    endpoints, variants = effect_ref.shape
    part = endpoints // 2
    own = variants * 2 // n
    lanes = held.shape[2]
    owner = lax.div(iota((part, lanes), 1), own) == iota((part, lanes), 0)
    fold = jnp.logical_and(
        lax.rem(iota((lanes, variants), 0), own) == lax.rem(iota((lanes, variants), 1), own),
        iota((lanes, variants), 0) < own * part,
    ).astype(F32).astype(BF16)
    column = lax.div(iota((endpoints, variants), 1), own)
    for which, out in enumerate((effect_ref, zscore_ref)):
        tall = jnp.concatenate([jnp.where(owner, held[k, which : which + 1, :], 0.0) for k in range(n)], axis=0)
        parts = [jnp.dot(third.astype(BF16), fold, preferred_element_type=F32) for third in thirds(tall)]
        tall = (parts[0] + parts[1]) + parts[2]
        result = jnp.zeros((endpoints, variants), F32)
        for c in range(n // 2):
            result = jnp.where(column == c, tall[c * endpoints : (c + 1) * endpoints], result)
        out[...] = result


def solution(mesh):
    n = mesh.shape["smp"]

    def body(dosage, flags, events, offsets):
        rows, columns = dosage.shape
        endpoints = offsets.shape[1]
        variants = flags.shape[0]
        own = variants * 2 // n
        part = endpoints // 2
        lanes = -(-own * part // 128) * 128
        out = jax.ShapeDtypeStruct((endpoints, variants), F32)
        held = pl.pallas_call(
            functools.partial(kernel, n),
            out_shape=jax.ShapeDtypeStruct((n, 2, lanes), F32),
            in_specs=[pl.BlockSpec(memory_space=pl.ANY)] * 4,
            out_specs=pl.BlockSpec(memory_space=pltpu.VMEM),
            scratch_shapes=[
                pltpu.VMEM((1, variants), jnp.int32),
                pltpu.VMEM((rows, columns), BF16),
                pltpu.VMEM((endpoints, rows), F32),
                pltpu.VMEM((endpoints, rows), jnp.int32),
                pltpu.VMEM((n, own + 2 * part, rows), F32),
                pltpu.VMEM((n, own + 2 * part, rows), F32),
                pltpu.VMEM((n * rows, lanes), F32),
                pltpu.VMEM((n * rows, lanes), F32),
                pltpu.VMEM((n * rows, lanes), F32),
                pltpu.VMEM((n * rows, lanes), F32),
                pltpu.VMEM((n * SUB, 4 * lanes), F32),
                pltpu.VMEM((n * SUB, 4 * lanes), F32),
                pltpu.VMEM((2, lanes), F32),
                pltpu.VMEM((n, 2, lanes), F32),
                pltpu.SemaphoreType.DMA((4,)),
            ]
            + [pltpu.SemaphoreType.DMA((n,))] * 4,
            compiler_params=pltpu.CompilerParams(collective_id=0, has_side_effects=True),
        )(flags.reshape(1, variants), dosage, offsets.T, events.T)
        return pl.pallas_call(
            functools.partial(unfold, n),
            out_shape=(out, out),
            in_specs=[pl.BlockSpec(memory_space=pltpu.VMEM)],
            out_specs=[pl.BlockSpec(memory_space=pltpu.VMEM)] * 2,
        )(held)

    return jax.shard_map(
        body,
        mesh=mesh,
        in_specs=(P("smp", "grp"), P("grp"), P("smp", "grp"), P("smp", "grp")),
        out_specs=(P(None, "grp"), P(None, "grp")),
        check_vma=False,
    )
```

profile of v0, /device:TPU:0, one launch (start us, length us, event | category | flops | bytes accessed | tf_op | source)
XLA Modules:
  0.0 25.7 jit_solution(10490633077301856886)
XLA Ops:
  0.6 23.5 %shard_map.59.held = f32[16,2,128]{2,1,0:T(2,128)} custom-call(s32[1,128]{1,0:T(1,128)} %bitcast.5, bf16[128,2048]{1,0:T(8,128)(2,1)} %dosage_hbm.1, f32[16,128]{1,0:T(8,128)} %bitcast.3, s32[16,128]{1,0:T(8,128)} %bitcast.4), custom_call_target="tpu_custom_call" | custom-call | tf_op jit(solution)/shard_map/pallas_call | solution.py:268
  24.1 1.5 %shard_map.60 = (f32[16,128]{1,0:T(8,128)}, f32[16,128]{1,0:T(8,128)}) custom-call(f32[16,2,128]{2,1,0:T(2,128)} %shard_map.59.held), custom_call_target="tpu_custom_call" | custom-call | tf_op jit(solution)/shard_map/pallas_call | solution.py:293
where the time goes:
time: 26 us; the launch traced here: 25.7 us
  Pallas kernels  25 us (96%)
  between operations  0.64 us (2%)
    pallas_call x1, Pallas kernels, body(): pl.pallas_call(functools.partial(kernel, n), out_shape=jax.ShapeDtypeStru...  23.5 us
    pallas_call x1, Pallas kernels, body(): pl.pallas_call(functools.partial(unfold, n), out_shape=(out, out), in_spe...  1.53 us

commit v1 on v0

v1 whole, which is shorter than its diff:
```python
import functools

import jax
import jax.numpy as jnp
from jax import lax
from jax.experimental import pallas as pl
from jax.experimental.pallas import tpu as pltpu
from jax.sharding import PartitionSpec as P

ITERS = 3
SUB = 8
LIMIT = 48 * 2**20
GROUP = 3
LOG2E = 1.4426950408889634
MESH = pl.DeviceIdType.MESH
F32 = jnp.float32
BF16 = jnp.bfloat16


def thirds(x):
    high = x.astype(BF16).astype(F32)
    rest = x - high
    middle = rest.astype(BF16).astype(F32)
    return high, middle, rest - middle


def transposed_dot(a, b):
    return lax.dot_general(a, b, (((0,), (0,)), ((), ())), preferred_element_type=F32)


def iota(shape, dim):
    return lax.broadcasted_iota(jnp.int32, shape, dim)


def kernel(
    n, flags_hbm, dosage_hbm, offsets_hbm, events_hbm, held,
    flags_ref, dosage_ref, offsets_ref, events_ref,
    send, recv, dose_ref, shift_ref, mark_ref, sums_ref, even_ref, odd_ref, rsend,
    load_sem, send_sem, recv_sem, rsend_sem, rrecv_sem,
):
    me = lax.axis_index("smp")
    rows, columns = dosage_ref.shape
    endpoints = offsets_ref.shape[0]
    part = endpoints // 2
    variants = flags_ref.shape[1]
    own = variants * 2 // n
    lanes = dose_ref.shape[1]
    steps = rows // SUB
    low = lax.convert_element_type(me < n // 2, jnp.int32)

    def far(at):
        up = at + lax.convert_element_type(at >= me, jnp.int32)
        down = n - 1 - at
        down = down - lax.convert_element_type(down <= me, jnp.int32)
        return low * down + (1 - low) * up

    loads = [
        pltpu.make_async_copy(src, dst, load_sem.at[at])
        for at, (src, dst) in enumerate(
            ((flags_hbm, flags_ref), (dosage_hbm, dosage_ref), (offsets_hbm, offsets_ref), (events_hbm, events_ref))
        )
    ]
    for load in loads:
        load.start()

    barrier = pltpu.get_barrier_semaphore()
    for at in range(n - 1):
        pl.semaphore_signal(barrier, inc=1, device_id={"smp": far(at)}, device_id_type=MESH)

    line = iota((rows, rows), 1)
    order = (iota((rows, rows), 0) == lax.rem(line, SUB) * steps + lax.div(line, SUB)).astype(F32).astype(BF16)

    loads[2].wait()
    loads[3].wait()
    four = jnp.concatenate([*thirds(offsets_ref[...] * LOG2E), events_ref[...].astype(F32)], axis=0)
    four = jnp.dot(four.astype(BF16), order, preferred_element_type=F32)
    high, middle, low_part, events = (four[k * endpoints : (k + 1) * endpoints] for k in range(4))
    offsets = (high + middle) + low_part
    for k in range(n):
        for at, values in ((own, offsets), (own + part, events)):
            send[k, pl.ds(at, part), :] = values[k % 2 * part : (k % 2 + 1) * part]

    loads[0].wait()
    chosen = (iota((columns, variants), 0) == flags_ref[...]).astype(F32).astype(BF16)
    loads[1].wait()
    genotype = jnp.dot(dosage_ref[...], chosen, preferred_element_type=F32).astype(BF16)
    genotype = transposed_dot(genotype, order)
    for k in range(n):
        send[k, pl.ds(0, own), :] = genotype[k // 2 * own : (k // 2 + 1) * own]

    pl.semaphore_wait(barrier, n - 1)

    def copy(at, slot):
        return pltpu.make_async_remote_copy(
            src_ref=send.at[at], dst_ref=recv.at[slot], send_sem=send_sem.at[0], recv_sem=recv_sem.at[slot],
            device_id={"smp": at}, device_id_type=MESH,
        )

    def rcopy(at):
        return pltpu.make_async_remote_copy(
            src_ref=rsend, dst_ref=held.at[me], send_sem=rsend_sem.at[0], recv_sem=rrecv_sem.at[0],
            device_id={"smp": at}, device_id_type=MESH,
        )

    for at in range(n - 1):
        copy(far(at), me).start()

    lane_e = iota((part, lanes), 1)
    lane_v = iota((own, lanes), 1)
    spread_e = (lax.div(lane_e, own) == iota((part, lanes), 0)).astype(F32)
    spread_v = jnp.logical_and(lax.rem(lane_v, own) == iota((own, lanes), 0), lane_v < own * part).astype(F32)
    none_e, none_v = jnp.zeros_like(spread_e), jnp.zeros_like(spread_v)
    spread = jnp.concatenate(
        [jnp.concatenate([none_v, none_v, spread_v], axis=1)]
        + [jnp.concatenate([spread_e, none_e, none_e], axis=1)] * 3
        + [jnp.concatenate([none_e, spread_e, none_e], axis=1)],
        axis=0,
    ).astype(BF16)

    def tile(block, t):
        return pl.ds(pl.multiple_of(block * rows + t * SUB, SUB), SUB)

    def moments(weight, dose, total, into, base):
        for k in range(4):
            total[k] = total[k] + weight
            into[base, pl.ds(k * lanes, lanes)] = total[k]
            if k < 3:
                weight = weight * dose

    zero = jnp.zeros((SUB, lanes), F32)

    def expand(slots, pieces, marked):
        mixed = []
        for values in pieces:
            doses, samples, events = values[:own], values[own : own + part], values[own + part :]
            tall = jnp.concatenate([doses, *thirds(samples), events], axis=0)
            mixed.append(transposed_dot(tall.astype(BF16), spread))
        for slot, values in zip(slots, mixed):
            total = [zero] * 4
            for t in reversed(range(steps)):
                shift, mark, dose = (values[t * SUB : (t + 1) * SUB, k * lanes : (k + 1) * lanes] for k in range(3))
                at = tile(slot, t)
                shift_ref[at, :] = shift
                mark_ref[at, :] = mark
                dose_ref[at, :] = dose
                marked = marked + mark * dose
                moments(jnp.exp2(shift), dose, total, sums_ref, at)
        return marked

    group = max(size for size in range(1, GROUP + 1) if (n - 1) % size == 0)

    def arrive(step, marked):
        slots = [far(n - 2 - (step * group + at)) for at in range(group)]
        for slot in slots:
            copy(slot, slot).wait_recv()
        return expand(slots, [recv[slot] for slot in slots], marked)

    marked = expand([me], [send[me]], zero)
    marked = lax.fori_loop(0, (n - 1) // group, arrive, marked)

    below = iota((SUB, lanes), 0)

    def scan(total, later):
        carry, fresh = [], []
        for x, run in zip(total, later):
            e = jnp.where(below < SUB - 1, pltpu.roll(x, SUB - 1, 0), 0.0)
            for shift in (1, 2, 4):
                e = e + jnp.where(below < SUB - shift, pltpu.roll(e, SUB - shift, 0), 0.0)
            carry.append(e + run)
            fresh.append(run + jnp.broadcast_to((x + e)[0:1], (SUB, lanes)))
        return carry, fresh

    def add_moments(block, slope, into):
        total = [zero] * 4
        for t in reversed(range(steps)):
            at = tile(block, t)
            dose = dose_ref[at, :]
            moments(jnp.exp2(shift_ref[at, :] + slope * dose), dose, total, into, pl.ds(t * SUB, SUB))
        return total

    def add_terms(block, source, base, carry, sums):
        first_sum, information, skewness = sums
        for t in reversed(range(steps)):
            here = pl.ds(base + t * SUB, SUB) if isinstance(base, int) else tile(base, t)
            s0, s1, s2, s3 = (source[here, pl.ds(k * lanes, lanes)] + carry[k] for k in range(4))
            mark = mark_ref[tile(block, t), :]
            inverse = 1.0 / s0
            scaled = mark * inverse
            first = s1 * inverse
            one = mark * first
            two = s2 * scaled
            spread = two - one * first
            first_sum = first_sum + one
            information = information + spread
            skewness = skewness + (s3 * scaled - first * (two + (spread + spread)))
        return first_sum, information, skewness

    def finish(effect, sums):
        first_sum, information, skewness = sums
        score, information, skewness = (
            jnp.sum(x, axis=0, keepdims=True) for x in (marked - first_sum, information, skewness)
        )
        effect = effect + (score + 0.5 * skewness / information) / information
        return effect, effect * jnp.sqrt(information)

    zeros = (zero,) * 3

    def opening(at, state):
        later, sums = state
        block = n - 1 - at
        total = [sums_ref[tile(block, 0), pl.ds(k * lanes, lanes)] for k in range(4)]
        carry, later = scan(total, later)
        return tuple(later), add_terms(block, sums_ref, block, carry, sums)

    _, sums = lax.fori_loop(0, n, opening, ((zero,) * 4, zeros), unroll=2)
    effect, zscore = finish(jnp.zeros((1, lanes), F32), sums)

    def sweep(_, state):
        effect, _ = state
        slope = jnp.broadcast_to(effect * LOG2E, (SUB, lanes))
        carry, later = scan(add_moments(n - 1, slope, even_ref), [zero] * 4)

        def pair(at, state):
            carry, later, sums = state
            block = n - 1 - 2 * at
            total = add_moments(block - 1, slope, odd_ref)
            sums = add_terms(block, even_ref, 0, carry, sums)
            carry, later = scan(total, later)
            total = add_moments(block - 2, slope, even_ref)
            sums = add_terms(block - 1, odd_ref, 0, carry, sums)
            carry, later = scan(total, later)
            return tuple(carry), tuple(later), sums

        carry, later, sums = lax.fori_loop(0, n // 2 - 1, pair, (tuple(carry), tuple(later), zeros))
        total = add_moments(0, slope, odd_ref)
        sums = add_terms(1, even_ref, 0, carry, sums)
        carry, _ = scan(total, later)
        return finish(effect, add_terms(0, odd_ref, 0, carry, sums))

    effect, zscore = lax.fori_loop(0, ITERS - 1, sweep, (effect, zscore))

    rsend[0:1, :] = effect
    rsend[1:2, :] = zscore

    for at in range(n - 1):
        rcopy(far(at)).start()

    mine = pltpu.make_async_copy(rsend, held.at[me], load_sem.at[0])
    mine.start()
    pltpu.make_async_copy(send.at[pl.ds(0, n - 1)], recv.at[pl.ds(0, n - 1)], send_sem.at[0]).wait()
    mine.wait()
    whole = held.at[pl.ds(0, n - 1)]
    pltpu.make_async_copy(whole, whole, rrecv_sem.at[0]).wait()
    pltpu.make_async_copy(whole, whole, rsend_sem.at[0]).wait()


def unfold(n, held, effect_ref, zscore_ref):
    endpoints, variants = effect_ref.shape
    part = endpoints // 2
    own = variants * 2 // n
    lanes = held.shape[2]
    owner = lax.div(iota((part, lanes), 1), own) == iota((part, lanes), 0)
    fold = jnp.logical_and(
        lax.rem(iota((lanes, variants), 0), own) == lax.rem(iota((lanes, variants), 1), own),
        iota((lanes, variants), 0) < own * part,
    ).astype(F32).astype(BF16)
    column = lax.div(iota((endpoints, variants), 1), own)
    for which, out in enumerate((effect_ref, zscore_ref)):
        tall = jnp.concatenate([jnp.where(owner, held[k, which : which + 1, :], 0.0) for k in range(n)], axis=0)
        parts = [jnp.dot(third.astype(BF16), fold, preferred_element_type=F32) for third in thirds(tall)]
        tall = (parts[0] + parts[1]) + parts[2]
        result = jnp.zeros((endpoints, variants), F32)
        for c in range(n // 2):
            result = jnp.where(column == c, tall[c * endpoints : (c + 1) * endpoints], result)
        out[...] = result


def solution(mesh):
    n = mesh.shape["smp"]

    def body(dosage, flags, events, offsets):
        rows, columns = dosage.shape
        endpoints = offsets.shape[1]
        variants = flags.shape[0]
        own = variants * 2 // n
        part = endpoints // 2
        lanes = -(-own * part // 128) * 128
        out = jax.ShapeDtypeStruct((endpoints, variants), F32)
        held = pl.pallas_call(
            functools.partial(kernel, n),
            out_shape=jax.ShapeDtypeStruct((n, 2, lanes), F32),
            in_specs=[pl.BlockSpec(memory_space=pl.ANY)] * 4,
            out_specs=pl.BlockSpec(memory_space=pl.ANY),
            scratch_shapes=[
                pltpu.VMEM((1, variants), jnp.int32),
                pltpu.VMEM((rows, columns), BF16),
                pltpu.VMEM((endpoints, rows), F32),
                pltpu.VMEM((endpoints, rows), jnp.int32),
                pltpu.VMEM((n, own + 2 * part, rows), F32),
                pltpu.VMEM((n, own + 2 * part, rows), F32),
                pltpu.VMEM((n * rows, lanes), F32),
                pltpu.VMEM((n * rows, lanes), F32),
                pltpu.VMEM((n * rows, lanes), F32),
                pltpu.VMEM((n * rows, 4 * lanes), F32),
                pltpu.VMEM((rows, 4 * lanes), F32),
                pltpu.VMEM((rows, 4 * lanes), F32),
                pltpu.VMEM((2, lanes), F32),
                pltpu.SemaphoreType.DMA((4,)),
                pltpu.SemaphoreType.DMA((1,)),
                pltpu.SemaphoreType.DMA((n,)),
                pltpu.SemaphoreType.DMA((1,)),
                pltpu.SemaphoreType.DMA((1,)),
            ],
            compiler_params=pltpu.CompilerParams(collective_id=0, has_side_effects=True, vmem_limit_bytes=LIMIT),
        )(*(pltpu.with_memory_space_constraint(x, pltpu.HBM) for x in (flags.reshape(1, variants), dosage, offsets.T, events.T)))
        return pl.pallas_call(
            functools.partial(unfold, n),
            out_shape=(out, out),
            in_specs=[pl.BlockSpec(memory_space=pltpu.VMEM)],
            out_specs=[pl.BlockSpec(memory_space=pltpu.VMEM)] * 2,
            compiler_params=pltpu.CompilerParams(vmem_limit_bytes=LIMIT // 8),
        )(held)

    return jax.shard_map(
        body,
        mesh=mesh,
        in_specs=(P("smp", "grp"), P("grp"), P("smp", "grp"), P("smp", "grp")),
        out_specs=(P(None, "grp"), P(None, "grp")),
        check_vma=False,
    )
```

time: 26 us -> 22.6 us (0.87)
  Pallas kernels: 25 us -> 21.8 us
    pallas_call x1, Pallas kernels: 23.5 us -> 21 us  [body(): pl.pallas_call(functools.partial(kernel, n), out_shape=jax.ShapeDtypeStru...]
    pallas_call x1, Pallas kernels: 1.53 us -> 0.81 us  [body(): pl.pallas_call(functools.partial(unfold, n), out_shape=(out, out), in_spe...]
where the time goes in v1:
time: 22.6 us; the launch traced here: 22.5 us
  Pallas kernels  21.8 us (96%)
  between operations  0.64 us (3%)
    pallas_call x1, Pallas kernels, body(): pl.pallas_call(functools.partial(kernel, n), out_shape=jax.ShapeDtypeStru...  21 us
    pallas_call x1, Pallas kernels, body(): pl.pallas_call(functools.partial(unfold, n), out_shape=(out, out), in_spe...  0.81 us

profile of v1, /device:TPU:0, one launch (start us, length us, event | category | flops | bytes accessed | tf_op | source)
XLA Modules:
  0.0 22.5 jit_solution(5794604967219199803)
XLA Ops:
  0.6 21.0 %shard_map.59.held = f32[16,2,128]{2,1,0:T(2,128)S(1)} custom-call(s32[1,128]{1,0:T(1,128)} %bitcast.5, bf16[128,2048]{1,0:T(8,128)(2,1)} %dosage_hbm.1, f32[16,128]{1,0:T(8,128)} %bitcast.3, s32[16,128]{1,0:T(8,128)} %bitcast.4), custom_call_target="tpu_custom_call" | custom-call | tf_op jit(solution)/shard_map/pallas_call | solution.py:289
  21.7 0.8 %shard_map.60 = (f32[16,128]{1,0:T(8,128)}, f32[16,128]{1,0:T(8,128)}) custom-call(f32[16,2,128]{2,1,0:T(2,128)S(1)} %shard_map.59.held), custom_call_target="tpu_custom_call" | custom-call | tf_op jit(solution)/shard_map/pallas_call | solution.py:316

commit v2 on v1

--- a/solution.py
+++ b/solution.py
@@ -1,4 +1,5 @@
 import functools
+import math
 
 import jax
 import jax.numpy as jnp
@@ -10,7 +11,6 @@
 ITERS = 3
 SUB = 8
 LIMIT = 48 * 2**20
-GROUP = 3
 LOG2E = 1.4426950408889634
 MESH = pl.DeviceIdType.MESH
 F32 = jnp.float32
@@ -35,8 +35,8 @@
 def kernel(
     n, flags_hbm, dosage_hbm, offsets_hbm, events_hbm, held,
     flags_ref, dosage_ref, offsets_ref, events_ref,
-    send, recv, dose_ref, shift_ref, mark_ref, sums_ref, even_ref, odd_ref, rsend,
-    load_sem, send_sem, recv_sem, rsend_sem, rrecv_sem,
+    send, recv, dose_ref, shift_ref, mark_ref, sums_ref, even_ref, odd_ref, state_ref, rsend,
+    load_sem, send_sem, recv_sem, rsend_sem, rrecv_sem, up,
 ):
     me = lax.axis_index("smp")
     rows, columns = dosage_ref.shape
@@ -46,13 +46,13 @@
     own = variants * 2 // n
     lanes = dose_ref.shape[1]
     steps = rows // SUB
-    low = lax.convert_element_type(me < n // 2, jnp.int32)
-
-    def far(at):
-        up = at + lax.convert_element_type(at >= me, jnp.int32)
-        down = n - 1 - at
-        down = down - lax.convert_element_type(down <= me, jnp.int32)
-        return low * down + (1 - low) * up
+    size = math.isqrt(n)
+    planes = n // size
+    plane, spot = lax.div(me, size), lax.rem(me, size)
+    final = plane == planes - 1
+
+    def others(at):
+        return at + lax.convert_element_type(at >= me, jnp.int32)
 
     loads = [
         pltpu.make_async_copy(src, dst, load_sem.at[at])
@@ -64,8 +64,31 @@
         load.start()
 
     barrier = pltpu.get_barrier_semaphore()
-    for at in range(n - 1):
-        pl.semaphore_signal(barrier, inc=1, device_id={"smp": far(at)}, device_id_type=MESH)
+
+    def member(plane, at):
+        return plane * size + lax.rem(spot + at, size)
+
+    def signal(sem, at):
+        pl.semaphore_signal(sem, inc=1, device_id={"smp": at}, device_id_type=MESH)
+
+    @pl.when(final)
+    def _():
+        for at in range(1, size):
+            signal(barrier, member(plane, at))
+
+    @pl.when(jnp.logical_not(final))
+    def _():
+        for at in range(n - 1):
+            signal(barrier, others(n - 2 - at))
+
+    def meet():
+        pl.semaphore_wait(barrier, n - 1)
+        for at in range(n - size):
+            signal(up.at[0], at)
+
+    @pl.when(jnp.logical_and(final, spot >= size // 2))
+    def _():
+        meet()
 
     line = iota((rows, rows), 1)
     order = (iota((rows, rows), 0) == lax.rem(line, SUB) * steps + lax.div(line, SUB)).astype(F32).astype(BF16)
@@ -88,7 +111,13 @@
     for k in range(n):
         send[k, pl.ds(0, own), :] = genotype[k // 2 * own : (k // 2 + 1) * own]
 
-    pl.semaphore_wait(barrier, n - 1)
+    @pl.when(jnp.logical_and(final, spot < size // 2))
+    def _():
+        meet()
+
+    @pl.when(jnp.logical_not(final))
+    def _():
+        pl.semaphore_wait(barrier, n - 1 - size)
 
     def copy(at, slot):
         return pltpu.make_async_remote_copy(
@@ -102,8 +131,22 @@
             device_id={"smp": at}, device_id_type=MESH,
         )
 
-    for at in range(n - 1):
-        copy(far(at), me).start()
+    for group in reversed(range(1, planes - 1)):
+
+        @pl.when(plane < group)
+        def _():
+            for at in range(size):
+                copy(member(group, at), me).start()
+
+    for at in range(1, size):
+        copy(member(plane, at), me).start()
+
+    for group in range(planes - 1):
+
+        @pl.when(plane > group)
+        def _():
+            for at in range(size):
+                copy(member(group, at), me).start()
 
     lane_e = iota((part, lanes), 1)
     lane_v = iota((own, lanes), 1)
@@ -147,16 +190,22 @@
                 moments(jnp.exp2(shift), dose, total, sums_ref, at)
         return marked
 
-    group = max(size for size in range(1, GROUP + 1) if (n - 1) % size == 0)
-
-    def arrive(step, marked):
-        slots = [far(n - 2 - (step * group + at)) for at in range(group)]
+    marked = expand([me], [send[me]], zero)
+
+    @pl.when(jnp.logical_not(final))
+    def _():
+        pl.semaphore_wait(up.at[0], size)
+        for at in range(size):
+            copy(member(planes - 1, at), me).start()
+
+    def arrive(slots, marked):
         for slot in slots:
             copy(slot, slot).wait_recv()
         return expand(slots, [recv[slot] for slot in slots], marked)
 
-    marked = expand([me], [send[me]], zero)
-    marked = lax.fori_loop(0, (n - 1) // group, arrive, marked)
+    def arrive_plane(at, marked):
+        lower = lax.convert_element_type(at <= plane, jnp.int32)
+        return arrive([member(lower * (plane - at) + (1 - lower) * at, to) for to in range(size)], marked)
 
     below = iota((SUB, lanes), 0)
 
@@ -184,15 +233,13 @@
             here = pl.ds(base + t * SUB, SUB) if isinstance(base, int) else tile(base, t)
             s0, s1, s2, s3 = (source[here, pl.ds(k * lanes, lanes)] + carry[k] for k in range(4))
             mark = mark_ref[tile(block, t), :]
-            inverse = 1.0 / s0
-            scaled = mark * inverse
-            first = s1 * inverse
-            one = mark * first
-            two = s2 * scaled
-            spread = two - one * first
+            inverse = mark * (1.0 / s0)
+            one = s1 * inverse
+            two = s2 * inverse
+            spread = two - one * one
             first_sum = first_sum + one
             information = information + spread
-            skewness = skewness + (s3 * scaled - first * (two + (spread + spread)))
+            skewness = skewness + (s3 * inverse - one * (two + (spread + spread)))
         return first_sum, information, skewness
 
     def finish(effect, sums):
@@ -204,15 +251,38 @@
         return effect, effect * jnp.sqrt(information)
 
     zeros = (zero,) * 3
-
-    def opening(at, state):
-        later, sums = state
-        block = n - 1 - at
-        total = [sums_ref[tile(block, 0), pl.ds(k * lanes, lanes)] for k in range(4)]
-        carry, later = scan(total, later)
-        return tuple(later), add_terms(block, sums_ref, block, carry, sums)
-
-    _, sums = lax.fori_loop(0, n, opening, ((zero,) * 4, zeros), unroll=2)
+    for k in range(7):
+        state_ref[k] = zero
+
+    def open_plane(group):
+        def opening(at, state):
+            block = group * size + size - 1 - at
+            total = [sums_ref[tile(block, 0), pl.ds(k * lanes, lanes)] for k in range(4)]
+            carry, later = scan(total, state[:4])
+            return (*later, *add_terms(block, sums_ref, block, carry, state[4:]))
+
+        state = lax.fori_loop(0, size, opening, tuple(state_ref[k] for k in range(7)), unroll=2)
+        for k in range(7):
+            state_ref[k] = state[k]
+
+    marked = arrive([member(plane, at) for at in range(1, size)], marked)
+
+    def arrive_plane(group, marked):
+        return arrive([member(group, at) for at in range(size)], marked)
+
+    marked = lax.fori_loop(plane + 1, planes, arrive_plane, marked)
+
+    @pl.loop(plane, planes)
+    def _(at):
+        open_plane(planes - 1 + plane - at)
+
+    def arrive_lower(at, marked):
+        marked = arrive_plane(plane - at, marked)
+        open_plane(plane - at)
+        return marked
+
+    marked = lax.fori_loop(1, plane + 1, arrive_lower, marked)
+    sums = [state_ref[4 + k] for k in range(3)]
     effect, zscore = finish(jnp.zeros((1, lanes), F32), sums)
 
     def sweep(_, state):
@@ -243,7 +313,7 @@
     rsend[1:2, :] = zscore
 
     for at in range(n - 1):
-        rcopy(far(at)).start()
+        rcopy(others(at)).start()
 
     mine = pltpu.make_async_copy(rsend, held.at[me], load_sem.at[0])
     mine.start()
@@ -304,12 +374,14 @@
                 pltpu.VMEM((n * rows, 4 * lanes), F32),
                 pltpu.VMEM((rows, 4 * lanes), F32),
                 pltpu.VMEM((rows, 4 * lanes), F32),
+                pltpu.VMEM((7, SUB, lanes), F32),
                 pltpu.VMEM((2, lanes), F32),
                 pltpu.SemaphoreType.DMA((4,)),
                 pltpu.SemaphoreType.DMA((1,)),
                 pltpu.SemaphoreType.DMA((n,)),
                 pltpu.SemaphoreType.DMA((1,)),
                 pltpu.SemaphoreType.DMA((1,)),
+                pltpu.SemaphoreType.REGULAR((1,)),
             ],
             compiler_params=pltpu.CompilerParams(collective_id=0, has_side_effects=True, vmem_limit_bytes=LIMIT),
         )(*(pltpu.with_memory_space_constraint(x, pltpu.HBM) for x in (flags.reshape(1, variants), dosage, offsets.T, events.T)))

time: 22.6 us -> 22.3 us (0.987)
  Pallas kernels: 21.8 us -> 21.5 us
    pallas_call x1, Pallas kernels: 21 us -> 20.7 us  [body(): pl.pallas_call(functools.partial(kernel, n), out_shape=jax.ShapeDtypeStru...]
where the time goes in v2:
time: 22.3 us; the launch traced here: 22.1 us
  Pallas kernels  21.5 us (96%)
  between operations  0.64 us (3%)
    pallas_call x1, Pallas kernels, body(): pl.pallas_call(functools.partial(kernel, n), out_shape=jax.ShapeDtypeStru...  20.7 us
    pallas_call x1, Pallas kernels, body(): pl.pallas_call(functools.partial(unfold, n), out_shape=(out, out), in_spe...  0.81 us

profile of v2, /device:TPU:0, one launch (start us, length us, event | category | flops | bytes accessed | tf_op | source)
XLA Modules:
  0.0 22.1 jit_solution(8886536444800894191)
XLA Ops:
  0.6 20.7 %shard_map.59.held = f32[16,2,128]{2,1,0:T(2,128)S(1)} custom-call(s32[1,128]{1,0:T(1,128)} %bitcast.5, bf16[128,2048]{1,0:T(8,128)(2,1)} %dosage_hbm.1, f32[16,128]{1,0:T(8,128)} %bitcast.3, s32[16,128]{1,0:T(8,128)} %bitcast.4), custom_call_target="tpu_custom_call" | custom-call | tf_op jit(solution)/shard_map/pallas_call | solution.py:359
  21.3 0.8 %shard_map.60 = (f32[16,128]{1,0:T(8,128)}, f32[16,128]{1,0:T(8,128)}) custom-call(f32[16,2,128]{2,1,0:T(2,128)S(1)} %shard_map.59.held), custom_call_target="tpu_custom_call" | custom-call | tf_op jit(solution)/shard_map/pallas_call | solution.py:388

commit v3 on v2

--- a/solution.py
+++ b/solution.py
@@ -36,7 +36,7 @@
     n, flags_hbm, dosage_hbm, offsets_hbm, events_hbm, held,
     flags_ref, dosage_ref, offsets_ref, events_ref,
     send, recv, dose_ref, shift_ref, mark_ref, sums_ref, even_ref, odd_ref, state_ref, rsend,
-    load_sem, send_sem, recv_sem, rsend_sem, rrecv_sem, up,
+    load_sem, send_sem, recv_sem, rsend_sem, rrecv_sem, relay_sem, up,
 ):
     me = lax.axis_index("smp")
     rows, columns = dosage_ref.shape
@@ -100,7 +100,7 @@
     high, middle, low_part, events = (four[k * endpoints : (k + 1) * endpoints] for k in range(4))
     offsets = (high + middle) + low_part
     for k in range(n):
-        for at, values in ((own, offsets), (own + part, events)):
+        for at, values in ((0, offsets), (part, events)):
             send[k, pl.ds(at, part), :] = values[k % 2 * part : (k % 2 + 1) * part]
 
     loads[0].wait()
@@ -109,7 +109,7 @@
     genotype = jnp.dot(dosage_ref[...], chosen, preferred_element_type=F32).astype(BF16)
     genotype = transposed_dot(genotype, order)
     for k in range(n):
-        send[k, pl.ds(0, own), :] = genotype[k // 2 * own : (k // 2 + 1) * own]
+        send[k, pl.ds(2 * part, own), :] = genotype[k // 2 * own : (k // 2 + 1) * own]
 
     @pl.when(jnp.logical_and(final, spot < size // 2))
     def _():
@@ -118,6 +118,11 @@
     @pl.when(jnp.logical_not(final))
     def _():
         pl.semaphore_wait(barrier, n - 1 - size)
+
+    doses_at = pl.ds(2 * part, send.shape[1] - 2 * part)
+    pair_at = pl.ds(0, 2 * part)
+    side = lax.rem(me, 2)
+    sibling = me + 1 - 2 * side
 
     def copy(at, slot):
         return pltpu.make_async_remote_copy(
@@ -125,6 +130,41 @@
             device_id={"smp": at}, device_id_type=MESH,
         )
 
+    def pair_copy(at, slot):
+        return pltpu.make_async_remote_copy(
+            src_ref=send.at[at, pair_at], dst_ref=recv.at[slot, pair_at], send_sem=send_sem.at[1],
+            recv_sem=recv_sem.at[slot], device_id={"smp": at}, device_id_type=MESH,
+        )
+
+    def relay(slot):
+        return pltpu.make_async_remote_copy(
+            src_ref=recv.at[slot, doses_at], dst_ref=recv.at[slot, doses_at], send_sem=send_sem.at[2],
+            recv_sem=relay_sem.at[slot], device_id={"smp": sibling}, device_id_type=MESH,
+        )
+
+    def shared(group):
+        return jnp.logical_and(group - plane < planes - 1, plane - group < planes - 1)
+
+    def same(group, at):
+        return group * size + 2 * lax.rem(lax.div(spot, 2) + at, size // 2) + side
+
+    def cross(group, at):
+        return group * size + 2 * lax.rem(lax.div(spot, 2) + at, size // 2) + 1 - side
+
+    def post(group):
+        for at in range(size // 2):
+            copy(same(group, at), me).start()
+
+        @pl.when(shared(group))
+        def _():
+            for at in range(size // 2):
+                pair_copy(cross(group, at), me).start()
+
+        @pl.when(jnp.logical_not(shared(group)))
+        def _():
+            for at in range(size // 2):
+                copy(cross(group, at), me).start()
+
     def rcopy(at):
         return pltpu.make_async_remote_copy(
             src_ref=rsend, dst_ref=held.at[me], send_sem=rsend_sem.at[0], recv_sem=rrecv_sem.at[0],
@@ -135,8 +175,7 @@
 
         @pl.when(plane < group)
         def _():
-            for at in range(size):
-                copy(member(group, at), me).start()
+            post(group)
 
     for at in range(1, size):
         copy(member(plane, at), me).start()
@@ -145,8 +184,7 @@
 
         @pl.when(plane > group)
         def _():
-            for at in range(size):
-                copy(member(group, at), me).start()
+            post(group)
 
     lane_e = iota((part, lanes), 1)
     lane_v = iota((own, lanes), 1)
@@ -175,7 +213,7 @@
     def expand(slots, pieces, marked):
         mixed = []
         for values in pieces:
-            doses, samples, events = values[:own], values[own : own + part], values[own + part :]
+            samples, events, doses = values[:part], values[part : 2 * part], values[2 * part : 2 * part + own]
             tall = jnp.concatenate([doses, *thirds(samples), events], axis=0)
             mixed.append(transposed_dot(tall.astype(BF16), spread))
         for slot, values in zip(slots, mixed):
@@ -195,17 +233,7 @@
     @pl.when(jnp.logical_not(final))
     def _():
         pl.semaphore_wait(up.at[0], size)
-        for at in range(size):
-            copy(member(planes - 1, at), me).start()
-
-    def arrive(slots, marked):
-        for slot in slots:
-            copy(slot, slot).wait_recv()
-        return expand(slots, [recv[slot] for slot in slots], marked)
-
-    def arrive_plane(at, marked):
-        lower = lax.convert_element_type(at <= plane, jnp.int32)
-        return arrive([member(lower * (plane - at) + (1 - lower) * at, to) for to in range(size)], marked)
+        post(planes - 1)
 
     below = iota((SUB, lanes), 0)
 
@@ -265,23 +293,60 @@
         for k in range(7):
             state_ref[k] = state[k]
 
-    marked = arrive([member(plane, at) for at in range(1, size)], marked)
-
-    def arrive_plane(group, marked):
-        return arrive([member(group, at) for at in range(size)], marked)
-
-    marked = lax.fori_loop(plane + 1, planes, arrive_plane, marked)
-
-    @pl.loop(plane, planes)
-    def _(at):
-        open_plane(planes - 1 + plane - at)
-
-    def arrive_lower(at, marked):
-        marked = arrive_plane(plane - at, marked)
-        open_plane(plane - at)
+    own_slots = [member(plane, at) for at in range(1, size)]
+    for slot in own_slots:
+        copy(slot, slot).wait_recv()
+    marked = expand(own_slots, [recv[slot] for slot in own_slots], marked)
+
+    @pl.when(final)
+    def _():
+        open_plane(plane)
+
+    def following(at):
+        lower = lax.convert_element_type(at > planes - 1 - plane, jnp.int32)
+        return lower * (planes - 1 - at) + (1 - lower) * (plane + at)
+
+    def settle(group, marked):
+        @pl.when(shared(group))
+        def _():
+            for at in range(size // 2):
+                slot = cross(group, at)
+                pair_copy(slot, slot).wait_recv()
+                relay(slot).wait_recv()
+
+        @pl.when(jnp.logical_not(shared(group)))
+        def _():
+            for at in range(size // 2):
+                for slot in (same(group, at), cross(group, at)):
+                    copy(slot, slot).wait_recv()
+
+        slots = [member(group, at) for at in range(size)]
+        marked = expand(slots, [recv[slot] for slot in slots], marked)
+
+        @pl.when(group == planes - 1)
+        def _():
+            @pl.loop(plane, planes)
+            def _(at):
+                open_plane(planes - 1 + plane - at)
+
+        @pl.when(group < plane)
+        def _():
+            open_plane(group)
+
         return marked
 
-    marked = lax.fori_loop(1, plane + 1, arrive_lower, marked)
+    def forward(group):
+        @pl.when(shared(group))
+        def _():
+            for at in range(size // 2):
+                slot = same(group, at)
+                copy(slot, slot).wait_recv()
+                relay(slot).start()
+
+    for at in range(1, planes):
+        forward(jnp.where(at > plane, at, plane - at))
+
+    marked = lax.fori_loop(1, planes, lambda at, marked: settle(following(at), marked), marked)
     sums = [state_ref[4 + k] for k in range(3)]
     effect, zscore = finish(jnp.zeros((1, lanes), F32), sums)
 
@@ -317,7 +382,18 @@
 
     mine = pltpu.make_async_copy(rsend, held.at[me], load_sem.at[0])
     mine.start()
-    pltpu.make_async_copy(send.at[pl.ds(0, n - 1)], recv.at[pl.ds(0, n - 1)], send_sem.at[0]).wait()
+    edge = jnp.logical_or(plane == 0, final)
+    half = size // 2
+    for here, many in ((edge, planes - 2), (jnp.logical_not(edge), planes - 1)):
+
+        @pl.when(here)
+        def _():
+            full = pl.ds(0, n - 1 - many * half)
+            pltpu.make_async_copy(send.at[full], recv.at[full], send_sem.at[0]).wait()
+            for at, piece in ((1, pair_at), (2, doses_at)):
+                part_of = pl.ds(0, many * half)
+                pltpu.make_async_copy(send.at[part_of, piece], recv.at[part_of, piece], send_sem.at[at]).wait()
+
     mine.wait()
     whole = held.at[pl.ds(0, n - 1)]
     pltpu.make_async_copy(whole, whole, rrecv_sem.at[0]).wait()
@@ -355,6 +431,7 @@
         own = variants * 2 // n
         part = endpoints // 2
         lanes = -(-own * part // 128) * 128
+        held_rows = 2 * part + -(-own // SUB) * SUB
         out = jax.ShapeDtypeStruct((endpoints, variants), F32)
         held = pl.pallas_call(
             functools.partial(kernel, n),
@@ -366,8 +443,8 @@
                 pltpu.VMEM((rows, columns), BF16),
                 pltpu.VMEM((endpoints, rows), F32),
                 pltpu.VMEM((endpoints, rows), jnp.int32),
-                pltpu.VMEM((n, own + 2 * part, rows), F32),
-                pltpu.VMEM((n, own + 2 * part, rows), F32),
+                pltpu.VMEM((n, held_rows, rows), F32),
+                pltpu.VMEM((n, held_rows, rows), F32),
                 pltpu.VMEM((n * rows, lanes), F32),
                 pltpu.VMEM((n * rows, lanes), F32),
                 pltpu.VMEM((n * rows, lanes), F32),
@@ -377,10 +454,11 @@
                 pltpu.VMEM((7, SUB, lanes), F32),
                 pltpu.VMEM((2, lanes), F32),
                 pltpu.SemaphoreType.DMA((4,)),
-                pltpu.SemaphoreType.DMA((1,)),
+                pltpu.SemaphoreType.DMA((3,)),
                 pltpu.SemaphoreType.DMA((n,)),
                 pltpu.SemaphoreType.DMA((1,)),
                 pltpu.SemaphoreType.DMA((1,)),
+                pltpu.SemaphoreType.DMA((n,)),
                 pltpu.SemaphoreType.REGULAR((1,)),
             ],
             compiler_params=pltpu.CompilerParams(collective_id=0, has_side_effects=True, vmem_limit_bytes=LIMIT),

time: 22.3 us -> 21.2 us (0.951)
  Pallas kernels: 21.5 us -> 20.4 us
    pallas_call x1, Pallas kernels: 20.7 us -> 19.6 us  [body(): pl.pallas_call(functools.partial(kernel, n), out_shape=jax.ShapeDtypeStru...]
where the time goes in v3:
time: 21.2 us; the launch traced here: 21.1 us
  Pallas kernels  20.4 us (96%)
  between operations  0.64 us (3%)
    pallas_call x1, Pallas kernels, body(): pl.pallas_call(functools.partial(kernel, n), out_shape=jax.ShapeDtypeStru...  19.6 us
    pallas_call x1, Pallas kernels, body(): pl.pallas_call(functools.partial(unfold, n), out_shape=(out, out), in_spe...  0.81 us

profile of v3, /device:TPU:0, one launch (start us, length us, event | category | flops | bytes accessed | tf_op | source)
XLA Modules:
  0.0 21.1 jit_solution(7687524616262545284)
XLA Ops:
  0.6 19.6 %shard_map.59.held = f32[16,2,128]{2,1,0:T(2,128)S(1)} custom-call(s32[1,128]{1,0:T(1,128)} %bitcast.5, bf16[128,2048]{1,0:T(8,128)(2,1)} %dosage_hbm.1, f32[16,128]{1,0:T(8,128)} %bitcast.3, s32[16,128]{1,0:T(8,128)} %bitcast.4), custom_call_target="tpu_custom_call" | custom-call | tf_op jit(solution)/shard_map/pallas_call | solution.py:436
  20.3 0.8 %shard_map.60 = (f32[16,128]{1,0:T(8,128)}, f32[16,128]{1,0:T(8,128)}) custom-call(f32[16,2,128]{2,1,0:T(2,128)S(1)} %shard_map.59.held), custom_call_target="tpu_custom_call" | custom-call | tf_op jit(solution)/shard_map/pallas_call | solution.py:466

commit v4 on v3

--- a/solution.py
+++ b/solution.py
@@ -124,22 +124,32 @@
     side = lax.rem(me, 2)
     sibling = me + 1 - 2 * side
 
+    def lane_of(at, slot):
+        apart = lax.convert_element_type(lax.div(at, size) != lax.div(slot, size), jnp.int32)
+        return apart * lax.rem(at + slot, 2)
+
+    def take(sem, many, piece):
+        blocks = pl.ds(0, many)
+        pltpu.make_async_copy(send.at[blocks, piece], recv.at[blocks, piece], sem).wait()
+
+    every = pl.ds(0, send.shape[1])
+
     def copy(at, slot):
         return pltpu.make_async_remote_copy(
-            src_ref=send.at[at], dst_ref=recv.at[slot], send_sem=send_sem.at[0], recv_sem=recv_sem.at[slot],
+            src_ref=send.at[at], dst_ref=recv.at[slot], send_sem=send_sem.at[0], recv_sem=recv_sem.at[lane_of(at, slot), lax.div(slot, size)],
             device_id={"smp": at}, device_id_type=MESH,
         )
 
     def pair_copy(at, slot):
         return pltpu.make_async_remote_copy(
             src_ref=send.at[at, pair_at], dst_ref=recv.at[slot, pair_at], send_sem=send_sem.at[1],
-            recv_sem=recv_sem.at[slot], device_id={"smp": at}, device_id_type=MESH,
+            recv_sem=recv_sem.at[1, lax.div(slot, size)], device_id={"smp": at}, device_id_type=MESH,
         )
 
     def relay(slot):
         return pltpu.make_async_remote_copy(
             src_ref=recv.at[slot, doses_at], dst_ref=recv.at[slot, doses_at], send_sem=send_sem.at[2],
-            recv_sem=relay_sem.at[slot], device_id={"smp": sibling}, device_id_type=MESH,
+            recv_sem=relay_sem.at[lax.div(slot, size)], device_id={"smp": sibling}, device_id_type=MESH,
         )
 
     def shared(group):
@@ -190,20 +200,14 @@
     lane_v = iota((own, lanes), 1)
     spread_e = (lax.div(lane_e, own) == iota((part, lanes), 0)).astype(F32)
     spread_v = jnp.logical_and(lax.rem(lane_v, own) == iota((own, lanes), 0), lane_v < own * part).astype(F32)
-    none_e, none_v = jnp.zeros_like(spread_e), jnp.zeros_like(spread_v)
-    spread = jnp.concatenate(
-        [jnp.concatenate([none_v, none_v, spread_v], axis=1)]
-        + [jnp.concatenate([spread_e, none_e, none_e], axis=1)] * 3
-        + [jnp.concatenate([none_e, spread_e, none_e], axis=1)],
-        axis=0,
-    ).astype(BF16)
+    spread_e, spread_v = spread_e.astype(BF16), spread_v.astype(BF16)
 
     def tile(block, t):
         return pl.ds(pl.multiple_of(block * rows + t * SUB, SUB), SUB)
 
     def moments(weight, dose, total, into, base):
         for k in range(4):
-            total[k] = total[k] + weight
+            total[k] = weight if total[k] is None else total[k] + weight
             into[base, pl.ds(k * lanes, lanes)] = total[k]
             if k < 3:
                 weight = weight * dose
@@ -214,12 +218,15 @@
         mixed = []
         for values in pieces:
             samples, events, doses = values[:part], values[part : 2 * part], values[2 * part : 2 * part + own]
-            tall = jnp.concatenate([doses, *thirds(samples), events], axis=0)
-            mixed.append(transposed_dot(tall.astype(BF16), spread))
+            mixed.append((
+                transposed_dot(jnp.concatenate(thirds(samples), axis=0).astype(BF16), jnp.concatenate([spread_e] * 3, axis=0)),
+                transposed_dot(events.astype(BF16), spread_e),
+                transposed_dot(doses.astype(BF16), spread_v),
+            ))
         for slot, values in zip(slots, mixed):
-            total = [zero] * 4
+            total = [None] * 4
             for t in reversed(range(steps)):
-                shift, mark, dose = (values[t * SUB : (t + 1) * SUB, k * lanes : (k + 1) * lanes] for k in range(3))
+                shift, mark, dose = (value[t * SUB : (t + 1) * SUB] for value in values)
                 at = tile(slot, t)
                 shift_ref[at, :] = shift
                 mark_ref[at, :] = mark
@@ -235,20 +242,21 @@
         pl.semaphore_wait(up.at[0], size)
         post(planes - 1)
 
-    below = iota((SUB, lanes), 0)
+    line = iota((SUB, lanes), 0)
+    kept = [(line < SUB - shift).astype(F32) for shift in (1, 1, 2, 4)]
 
     def scan(total, later):
         carry, fresh = [], []
         for x, run in zip(total, later):
-            e = jnp.where(below < SUB - 1, pltpu.roll(x, SUB - 1, 0), 0.0)
-            for shift in (1, 2, 4):
-                e = e + jnp.where(below < SUB - shift, pltpu.roll(e, SUB - shift, 0), 0.0)
+            e = pltpu.roll(x, SUB - 1, 0) * kept[0]
+            for at, shift in ((1, 1), (2, 2), (3, 4)):
+                e = e + pltpu.roll(e, SUB - shift, 0) * kept[at]
             carry.append(e + run)
             fresh.append(run + jnp.broadcast_to((x + e)[0:1], (SUB, lanes)))
         return carry, fresh
 
     def add_moments(block, slope, into):
-        total = [zero] * 4
+        total = [None] * 4
         for t in reversed(range(steps)):
             at = tile(block, t)
             dose = dose_ref[at, :]
@@ -294,8 +302,7 @@
             state_ref[k] = state[k]
 
     own_slots = [member(plane, at) for at in range(1, size)]
-    for slot in own_slots:
-        copy(slot, slot).wait_recv()
+    take(recv_sem.at[0, plane], size - 1, every)
     marked = expand(own_slots, [recv[slot] for slot in own_slots], marked)
 
     @pl.when(final)
@@ -309,16 +316,13 @@
     def settle(group, marked):
         @pl.when(shared(group))
         def _():
-            for at in range(size // 2):
-                slot = cross(group, at)
-                pair_copy(slot, slot).wait_recv()
-                relay(slot).wait_recv()
+            take(recv_sem.at[1, group], size // 2, pair_at)
+            take(relay_sem.at[group], size // 2, doses_at)
 
         @pl.when(jnp.logical_not(shared(group)))
         def _():
-            for at in range(size // 2):
-                for slot in (same(group, at), cross(group, at)):
-                    copy(slot, slot).wait_recv()
+            take(recv_sem.at[0, group], size // 2, every)
+            take(recv_sem.at[1, group], size // 2, every)
 
         slots = [member(group, at) for at in range(size)]
         marked = expand(slots, [recv[slot] for slot in slots], marked)
@@ -338,10 +342,9 @@
     def forward(group):
         @pl.when(shared(group))
         def _():
+            take(recv_sem.at[0, group], size // 2, every)
             for at in range(size // 2):
-                slot = same(group, at)
-                copy(slot, slot).wait_recv()
-                relay(slot).start()
+                relay(same(group, at)).start()
 
     for at in range(1, planes):
         forward(jnp.where(at > plane, at, plane - at))
@@ -455,10 +458,10 @@
                 pltpu.VMEM((2, lanes), F32),
                 pltpu.SemaphoreType.DMA((4,)),
                 pltpu.SemaphoreType.DMA((3,)),
-                pltpu.SemaphoreType.DMA((n,)),
+                pltpu.SemaphoreType.DMA((2, n // math.isqrt(n))),
                 pltpu.SemaphoreType.DMA((1,)),
                 pltpu.SemaphoreType.DMA((1,)),
-                pltpu.SemaphoreType.DMA((n,)),
+                pltpu.SemaphoreType.DMA((n // math.isqrt(n),)),
                 pltpu.SemaphoreType.REGULAR((1,)),
             ],
             compiler_params=pltpu.CompilerParams(collective_id=0, has_side_effects=True, vmem_limit_bytes=LIMIT),

time: 21.2 us -> 21 us (level)
  no operation moved by 1% of the time
where the time goes in v4:
time: 21 us; the launch traced here: 20.9 us
  Pallas kernels  20.2 us (96%)
  between operations  0.64 us (3%)
    pallas_call x1, Pallas kernels, body(): pl.pallas_call(functools.partial(kernel, n), out_shape=jax.ShapeDtypeStru...  19.4 us
    pallas_call x1, Pallas kernels, body(): pl.pallas_call(functools.partial(unfold, n), out_shape=(out, out), in_spe...  0.81 us

profile of v4, /device:TPU:0, one launch (start us, length us, event | category | flops | bytes accessed | tf_op | source)
XLA Modules:
  0.0 20.9 jit_solution(13590572079793397661)
XLA Ops:
  0.6 19.4 %shard_map.59.held = f32[16,2,128]{2,1,0:T(2,128)S(1)} custom-call(s32[1,128]{1,0:T(1,128)} %bitcast.5, bf16[128,2048]{1,0:T(8,128)(2,1)} %dosage_hbm.1, f32[16,128]{1,0:T(8,128)} %bitcast.3, s32[16,128]{1,0:T(8,128)} %bitcast.4), custom_call_target="tpu_custom_call" | custom-call | tf_op jit(solution)/shard_map/pallas_call | solution.py:439
  20.1 0.8 %shard_map.60 = (f32[16,128]{1,0:T(8,128)}, f32[16,128]{1,0:T(8,128)}) custom-call(f32[16,2,128]{2,1,0:T(2,128)S(1)} %shard_map.59.held), custom_call_target="tpu_custom_call" | custom-call | tf_op jit(solution)/shard_map/pallas_call | solution.py:469

commit v5 on v4

--- a/solution.py
+++ b/solution.py
@@ -161,10 +161,11 @@
     def cross(group, at):
         return group * size + 2 * lax.rem(lax.div(spot, 2) + at, size // 2) + 1 - side
 
-    def post(group):
+    def post_same(group):
         for at in range(size // 2):
             copy(same(group, at), me).start()
 
+    def post_cross(group):
         @pl.when(shared(group))
         def _():
             for at in range(size // 2):
@@ -174,6 +175,10 @@
         def _():
             for at in range(size // 2):
                 copy(cross(group, at), me).start()
+
+    def post(group):
+        post_same(group)
+        post_cross(group)
 
     def rcopy(at):
         return pltpu.make_async_remote_copy(
@@ -187,14 +192,14 @@
         def _():
             post(group)
 
+    for group in range(planes - 1):
+
+        @pl.when(plane > group)
+        def _():
+            post(group)
+
     for at in range(1, size):
         copy(member(plane, at), me).start()
-
-    for group in range(planes - 1):
-
-        @pl.when(plane > group)
-        def _():
-            post(group)
 
     lane_e = iota((part, lanes), 1)
     lane_v = iota((own, lanes), 1)
@@ -346,10 +351,17 @@
             for at in range(size // 2):
                 relay(same(group, at)).start()
 
-    for at in range(1, planes):
-        forward(jnp.where(at > plane, at, plane - at))
-
-    marked = lax.fori_loop(1, planes, lambda at, marked: settle(following(at), marked), marked)
+    def nearest(at):
+        return jnp.where(at > plane, at, plane - at)
+
+    early = jnp.logical_and(final, side == 0)
+    forward(nearest(1))
+    marked = lax.cond(early, lambda marked: settle(following(1), marked), lambda marked: marked, marked)
+    for at in range(2, planes):
+        forward(nearest(at))
+
+    start = 1 + lax.convert_element_type(early, jnp.int32)
+    marked = lax.fori_loop(start, planes, lambda at, marked: settle(following(at), marked), marked)
     sums = [state_ref[4 + k] for k in range(3)]
     effect, zscore = finish(jnp.zeros((1, lanes), F32), sums)
 

time: 21 us -> 20.9 us (level)
  no operation moved by 1% of the time
where the time goes in v5:
time: 20.9 us; the launch traced here: 20.8 us
  Pallas kernels  20.2 us (97%)
  between operations  0.64 us (3%)
    pallas_call x1, Pallas kernels, body(): pl.pallas_call(functools.partial(kernel, n), out_shape=jax.ShapeDtypeStru...  19.4 us
    pallas_call x1, Pallas kernels, body(): pl.pallas_call(functools.partial(unfold, n), out_shape=(out, out), in_spe...  0.81 us

profile of v5, /device:TPU:0, one launch (start us, length us, event | category | flops | bytes accessed | tf_op | source)
XLA Modules:
  0.0 20.8 jit_solution(17675498348764497944)
XLA Ops:
  0.6 19.4 %shard_map.59.held = f32[16,2,128]{2,1,0:T(2,128)S(1)} custom-call(s32[1,128]{1,0:T(1,128)} %bitcast.5, bf16[128,2048]{1,0:T(8,128)(2,1)} %dosage_hbm.1, f32[16,128]{1,0:T(8,128)} %bitcast.3, s32[16,128]{1,0:T(8,128)} %bitcast.4), custom_call_target="tpu_custom_call" | custom-call | tf_op jit(solution)/shard_map/pallas_call | solution.py:451
  20.0 0.8 %shard_map.60 = (f32[16,128]{1,0:T(8,128)}, f32[16,128]{1,0:T(8,128)}) custom-call(f32[16,2,128]{2,1,0:T(2,128)S(1)} %shard_map.59.held), custom_call_target="tpu_custom_call" | custom-call | tf_op jit(solution)/shard_map/pallas_call | solution.py:481
